TPU v7x, 1024 devices: a whole 4x8x16 slice. The times are simulated.
1024 devices in a mesh: dp: 8 (over y), mp: 128 (over x, z, core).
Axes of the slice: x: 4, y: 8, z: 16, core: 2. Of those that a mesh axis runs over, the one named last changes fastest.
Arguments:
- inputs: bfloat16 [1024, 2560], P('dp'), may hold values from -6 to 6
- cotangent: bfloat16 [1024, 2560], P('dp'), may hold values from -6 to 6
- w_in: bfloat16 [128, 16, 128, 128], P('mp', 'dp'), may hold values from -0.125 to 0.125
- w_out: bfloat16 [128, 16, 128, 128], P('mp', 'dp'), may hold values from -0.0546875 to 0.0546875
- block_index: int32 [128, 16], P('mp'), may hold values from 0 to 19, as said below
- block_count: int32 [128], P('mp'), may hold values from 8 to 16, as said below
- drop_seeds: int32 [1024], P('dp'), may hold values from 0 to 1073741823
Outputs:
- outputs: bfloat16 [1024, 2560], P(('dp', 'mp'))
- input_grad: bfloat16 [1024, 2560], P(('dp', 'mp'))
- w_in_grad: float32 [128, 16, 128, 128], P('mp', 'dp')
- w_out_grad: float32 [128, 16, 128, 128], P('mp', 'dp')
Inputs may be any that keep to these rules, and one draw needn't show every extreme that they name: `block_index`: each row holds 16 different feature blocks; the first slots hold a few shared blocks and the blocks of a butterfly over the feature blocks. `block_count`: some hidden block uses all 16 slots and some uses 16 // 2.
All inputs are finite; a program needn't handle non-finite values.
Results may differ from a plain program's by a relative error of at most 0.012.
Values may be sent and summed in bfloat16 or wider, within the bound.
A program may use at most 32 MiB of HBM per device.

v0:
```python
import math

import jax
import jax.numpy as jnp
from jax import lax
from jax.sharding import PartitionSpec as P

BS = 128
K = 16


def scramble(value):
    value = value ^ lax.shift_right_logical(value, jnp.int32(16))
    value = value * jnp.int32(73244475)
    value = value ^ lax.shift_right_logical(value, jnp.int32(16))
    value = value * jnp.int32(73244475)
    value = value ^ lax.shift_right_logical(value, jnp.int32(16))
    return value


def keep_factor(seeds, first_unit):
    units = first_unit + jnp.arange(BS, dtype=jnp.int32)
    mixed = scramble(seeds[:, None] + units[None, :] * jnp.int32(668265261))
    kept = mixed & jnp.int32(7) != jnp.int32(0)
    return kept.astype(jnp.float32) * jnp.float32(8.0 / 7.0)


def gelu_parts(pre_act):
    coeff = math.sqrt(2.0 / math.pi)
    inner = coeff * (pre_act + 0.044715 * pre_act**3)
    tanh_val = jnp.tanh(inner)
    activation = 0.5 * pre_act * (1.0 + tanh_val)
    slope = 0.5 * (1.0 + tanh_val) + 0.5 * pre_act * (1.0 - tanh_val * tanh_val) * coeff * (
        1.0 + 3.0 * 0.044715 * pre_act * pre_act
    )
    return (activation, slope)


def place_blocks(blocks, idx_row, block_cols):
    tok_rows = blocks.shape[0]
    placed = jnp.zeros((tok_rows, block_cols, BS), jnp.float32).at[:, idx_row].set(blocks)
    return placed.reshape(tok_rows, block_cols * BS)


def spread(partial_value):
    return lax.psum_scatter(partial_value, "mp", scatter_dimension=0, tiled=True).astype(
        jnp.bfloat16
    )


def body(inputs, cotangent, w_in, w_out, block_index, block_count, drop_seeds):
    tok_rows, feat_width = inputs.shape
    block_cols = feat_width // BS
    w_first, w_second = (
        lax.all_gather(w_in, "dp", axis=1, tiled=True),
        lax.all_gather(w_out, "dp", axis=1, tiled=True),
    )
    idx_row = block_index[0]
    valid = jnp.arange(K, dtype=jnp.int32) < block_count[0]
    valid_half = valid.astype(jnp.bfloat16)
    valid_full = valid.astype(jnp.float32)
    w1m = w_first[0] * valid_half[:, None, None]
    w2m = w_second[0] * valid_half[:, None, None]
    selected = jnp.take(inputs.reshape(tok_rows, block_cols, BS), idx_row, axis=1)
    pre_act = jnp.einsum("tkc,kcf->tf", selected, w1m, preferred_element_type=jnp.float32)
    activation, slope = gelu_parts(pre_act)
    keep_scale = keep_factor(drop_seeds, lax.axis_index("mp") * BS)
    dropped = (activation * keep_scale).astype(jnp.bfloat16)
    out_blocks = jnp.einsum("tf,kfc->tkc", dropped, w2m, preferred_element_type=jnp.float32)
    out_part = place_blocks(out_blocks, idx_row, block_cols)
    outputs = spread(out_part)
    cot_sel = jnp.take(cotangent.reshape(tok_rows, block_cols, BS), idx_row, axis=1)
    grad_drop = jnp.einsum("tkc,kfc->tf", cot_sel, w2m, preferred_element_type=jnp.float32)
    grad_pre = (grad_drop * keep_scale * slope).astype(jnp.bfloat16)
    in_blocks = jnp.einsum("tf,kcf->tkc", grad_pre, w1m, preferred_element_type=jnp.float32)
    in_part = place_blocks(in_blocks, idx_row, block_cols)
    input_grad = spread(in_part)
    term_in = (
        jnp.einsum("tkc,tf->kcf", selected, grad_pre, preferred_element_type=jnp.float32)
        * valid_full[:, None, None]
    )
    term_out = (
        jnp.einsum("tf,tkc->kfc", dropped, cot_sel, preferred_element_type=jnp.float32)
        * valid_full[:, None, None]
    )
    grad_in, grad_out = (
        lax.psum_scatter(
            term_in.astype(jnp.bfloat16), "dp", scatter_dimension=0, tiled=True
        ).astype(jnp.float32),
        lax.psum_scatter(
            term_out.astype(jnp.bfloat16), "dp", scatter_dimension=0, tiled=True
        ).astype(jnp.float32),
    )
    return (outputs, input_grad, grad_in[None], grad_out[None])


def solution(mesh):
    placed = (
        P("dp", None),
        P("dp", None),
        P("mp", "dp", None, None),
        P("mp", "dp", None, None),
        P("mp", None),
        P("mp"),
        P("dp"),
    )
    return jax.shard_map(
        body,
        mesh=mesh,
        in_specs=placed,
        out_specs=(
            P(("dp", "mp"), None),
            P(("dp", "mp"), None),
            P("mp", "dp", None, None),
            P("mp", "dp", None, None),
        ),
        check_vma=False,
    )
```

profile of v0, /device:TPU:16, one launch (start us, length us, event | category | flops | bytes accessed | tf_op | source)
XLA Modules:
  0.0 619.1 jit_solution(9303654849714045700)
XLA Ops:
  7.2 0.7 compare_and_fusion
  7.9 0.7 compare_select_fusion
  9.2 36.0 %all_gather.6 = bf16[1,16,128,128]{3,2,0,1:T(8,128)(2,1)S(1)} all-gather(bf16[1,2,128,128]{3,2,0,1:T(8,128)(2,1)} %bitcast.78), channel_id=1, replica_groups=mesh['dp'=8,'mp'=128] {'dp'}, dimensions={1}, use_global_device_ids=true | all-gather | bytes 589824 | tf_op jit(solution)/shard_map/all_gather | solution.py:55
  45.3 1.5 copy.25
  46.8 0.3 copy.26
  47.1 0.3 copy.30
  47.4 0.3 copy.31
  47.8 0.7 gather_fusion
  48.4 0.6 gather_fusion.1
  49.1 0.4 convolution_bitcast_fusion.3
  49.5 1.4 fusion.2
  50.9 0.0 reduce-scatter.5.cloned.1.call-start
  50.9 25.4 %all_gather.7 = bf16[1,16,128,128]{3,2,0,1:T(8,128)(2,1)S(1)} all-gather(bf16[1,2,128,128]{3,2,0,1:T(8,128)(2,1)S(1)} %bitcast.79), channel_id=1, replica_groups=mesh['dp'=8,'mp'=128] {'dp'}, dimensions={1}, use_global_device_ids=true | all-gather | bytes 589824 | tf_op jit(solution)/shard_map/all_gather | solution.py:56
  76.3 0.4 fusion.6
  76.8 1.4 fusion
  78.2 0.4 convolution_bitcast_fusion.1
  78.6 1.4 convolution_bitcast_fusion
  79.9 0.1 broadcast.72.clone
  80.1 1.1 scatter_fusion
  81.2 0.4 copy.29
  81.6 0.1 broadcast.72.clone.1
  81.7 2.3 scatter_fusion.1
  84.0 1.5 copy.32
  85.5 518.9 %all-reduce.4 = (bf16[128,2560]{0,1:T(8,128)(2,1)S(1)}, bf16[128,2560]{0,1:T(8,128)(2,1)S(1)}) all-reduce(f32[128,2560]{0,1:T(8,128)S(1)} %bitcast.74, f32[128,2560]{0,1:T(8,128)} %bitcast.75), channel_id=2, replica_groups=mesh['dp'=8,'mp'=128] {'mp'}, use_global_device_ids=true, to_apply=%region_1.3.clone | all-reduce | flops 655360 | bytes 3932160
  604.4 1.3 dynamic-slice
  605.6 0.9 dynamic-slice_convert_fusion.1
  606.5 0.9 copy.35
  607.4 0.9 dynamic-slice_convert_fusion
  608.3 0.9 copy.36
  609.2 0.8 bitcast_convert_fusion
  610.0 0.8 copy.37
  610.8 1.5 bitcast_convert_fusion.1
  (17 shorter events, 0.1 us)
Async XLA Ops:
  7.2 602.0 %reduce-scatter.7.cloned.1.call-start = ((), (), s32[]{:S(2)}) async-start(), calls=%async_computation.3 | async-start | bytes 589824 | tf_op jit(solution)/shard_map/reduce_scatter | solution.py:90
  45.3 1.8 copy-start
  48.4 1.0 copy-start.2
  49.5 1.5 copy-start.1
  50.9 559.9 %reduce-scatter.5.cloned.1.call-start = ((), (), s32[]{:S(2)}) async-start(), calls=%async_computation.2 | async-start | bytes 589824 | tf_op jit(solution)/shard_map/reduce_scatter | solution.py:87
  76.7 1.4 copy-start.3
Sparse Core Ops, SparseCore 0:
  51.0 41.0 reduce-scatter.6
  95.9 43.9 reduce-scatter.4
where the time goes:
time: 620 us; the launch traced here: 619 us
  blocking collectives  580 us (94%)
  between operations  14.9 us (2%)
  local copies, waits for them, and re-layouts  14.8 us (2%)
    unnamed x1, blocking collectives  519 us
    all_gather x1, blocking collectives, body(): lax.all_gather(w_in, 'dp', axis=1, tiled=True)  36 us
    all_gather x1, blocking collectives, body(): lax.all_gather(w_out, 'dp', axis=1, tiled=True)  25.4 us
  transfers between devices with their start and end apart: 2, of which 0 were waited for; matrix products, arithmetic and copies ran while one was open for 2% of the time, Pallas kernels for 0%

commit v1 on v0

v1 whole, which is shorter than its diff:
```python
import math

import jax
import jax.numpy as jnp
from jax import lax
from jax.experimental import pallas as pl
from jax.experimental.pallas import tpu as pltpu
from jax.sharding import PartitionSpec as P

BS = 128
K = 16
NJ = 20
HJ = NJ // 2
NY = 8
NX = 4
NZ = 16
MESH = pl.DeviceIdType.MESH
F32 = jnp.float32
BF16 = jnp.bfloat16
Z_ORDER = (8, 7, 9, 6, 10, 5, 11, 4, 12, 3, 13, 2, 14, 1, 15)


def scramble(value):
    for _ in range(2):
        value = value ^ lax.shift_right_logical(value, jnp.int32(16))
        value = value * jnp.int32(73244475)
    return value ^ lax.shift_right_logical(value, jnp.int32(16))


def gelu_parts(pre_act):
    coeff = math.sqrt(2.0 / math.pi)
    square = pre_act * pre_act
    inner = coeff * (pre_act + 0.044715 * (square * pre_act))
    tanh_val = jnp.tanh(inner)
    activation = 0.5 * pre_act * (1.0 + tanh_val)
    slope = 0.5 * (1.0 + tanh_val) + 0.5 * pre_act * (1.0 - tanh_val * tanh_val) * coeff * (
        1.0 + 3.0 * 0.044715 * square
    )
    return activation, slope


def mm(a, b):
    return lax.dot_general(a, b, (((1,), (0,)), ((), ())), preferred_element_type=F32)


def mm_t(a, b):
    return lax.dot_general(a, b, (((1,), (1,)), ((), ())), preferred_element_type=F32)


def rdma(src, dst, send_sem, recv_sem, device):
    return pltpu.make_async_remote_copy(
        src_ref=src, dst_ref=dst, send_sem=send_sem, recv_sem=recv_sem,
        device_id=device, device_id_type=MESH,
    )


def ag_slots(step, way):
    return (0, 1) if step < NY // 2 else (way,)


def rs_slots(step, way):
    return (0, 1) if step > 1 else (way,)


def kernel(
    x_hbm, g_hbm, wi_hbm, wo_hbm, idx_ref, cnt_ref, seed_ref,
    out_ref, ing_ref, gwi_ref, gwo_ref,
    x3, g3, x3t, wg, keep_ref, perm_ref, pre_ref, gd_ref, dt_ref, gp_ref,
    rs_send, rs_recv, c_send, c_recv, own, x_send, x_recv, zsum, z_send, z_recv,
    idxv, inv,
    ld_sem, wl_sem, ag_ss, ag_rs, rs_ss, rs_rs, c_ss, c_rs, x_ss, x_rs, z_ss, z_rs, ready,
):
    y = lax.axis_index("dp")
    mp = lax.axis_index("mp")
    core = lax.rem(mp, 2)
    z = lax.rem(lax.div(mp, 2), NZ)
    x = lax.div(mp, 2 * NZ)

    def at(yy, xx, zz, cc):
        return (yy, (xx * NZ + zz) * 2 + cc)

    def wrap(value, size):
        return lax.rem(value + size, size)

    y_dev = (at(wrap(y + 1, NY), x, z, core), at(wrap(y - 1, NY), x, z, core))
    x_dev = (at(y, wrap(x + 1, NX), z, core), at(y, wrap(x - 1, NX), z, core))
    pair_dev = at(y, x, z, 1 - core)

    def z_dev(shift):
        return at(y, x, wrap(z + shift, NZ), core)

    w_hbm = (wi_hbm, wo_hbm)

    loads = []
    for j in range(NJ):
        cols = pl.ds(j * BS, BS)
        loads.append(pltpu.make_async_copy(x_hbm.at[:, cols], x3.at[j], ld_sem.at[0, j]))
        loads.append(pltpu.make_async_copy(g_hbm.at[:, cols], g3.at[j], ld_sem.at[1, j]))
    own_w = [
        pltpu.make_async_copy(w_hbm[w].at[0], wg.at[w, pl.ds(2 * y, 2)], wl_sem.at[w])
        for w in range(2)
    ]

    barrier = pltpu.get_barrier_semaphore()
    around = (*y_dev, *x_dev, z_dev(1), z_dev(-1), pair_dev)
    for device in around:
        pl.semaphore_signal(barrier, inc=1, device_id=device, device_id_type=MESH)
    for copy in own_w + loads:
        copy.start()
    pl.semaphore_wait(barrier, len(around))

    def ag_origin(step, way):
        return wrap(y - step if way == 0 else y + step, NY)

    def ag_copy(w, step, way, s):
        slot = 2 * ag_origin(step - 1, way) + s
        src = w_hbm[w].at[0, s] if step == 1 else wg.at[w, slot]
        return rdma(
            src, wg.at[w, slot], ag_ss.at[w, way, step - 1, s], ag_rs.at[w, way, step - 1, s],
            y_dev[way],
        )

    def ag_wait(w, step, way, s):
        here = wg.at[w, 2 * ag_origin(step, way) + s]
        rdma(
            here, here, ag_ss.at[w, way, step - 1, s], ag_rs.at[w, way, step - 1, s], y_dev[way]
        ).wait_recv()

    sends = []

    def start(copy):
        copy.start()
        sends.append(copy)

    for w in range(2):
        for s in range(2):
            for way in range(2):
                start(ag_copy(w, 1, way, s))

    for k in range(K):
        idxv[k] = jnp.where(k < cnt_ref[0], idx_ref[0, k], NJ)
    for j in range(NJ):
        found = jnp.int32(K)
        for k in range(K):
            found = jnp.where(idxv[k] == j, k, found)
        inv[j] = found
    blank = jnp.zeros((BS, BS), BF16)
    x3[NJ] = blank
    g3[NJ] = blank
    wg[0, K] = blank
    wg[1, K] = blank

    rows = lax.broadcasted_iota(jnp.int32, (BS, BS), 0)
    cols = lax.broadcasted_iota(jnp.int32, (BS, BS), 1)
    seeds = jnp.broadcast_to(seed_ref[...], (BS, BS)).T
    mixed = scramble(seeds + (mp * BS + cols) * jnp.int32(668265261))
    keep_ref[...] = jnp.where((mixed & 7) != 0, F32(8.0 / 7.0), F32(0.0))
    half = lax.shift_right_logical(rows, 6)
    tok_x = (x + (lax.shift_right_logical(rows, 4) & 3)) & 3
    tok_z = (z + (rows & 15)) & 15
    tok_c = jnp.where(half == 1, core, 1 - core)
    token = tok_x * 32 + tok_z * 2 + tok_c
    perm_ref[...] = jnp.where(token == cols, F32(1.0), F32(0.0)).astype(BF16)

    for copy in loads:
        copy.wait()

    def ready_round(r):
        for shift in (1 << r, -(1 << r)):
            pl.semaphore_signal(
                ready.at[r], inc=1, device_id=z_dev(shift), device_id_type=MESH
            )

    ready_round(0)
    for k in range(K):
        x3t[k] = x3[idxv[k]].T

    def two(ref, origin):
        return ref[idxv[2 * origin]], ref[idxv[2 * origin + 1]]

    def pre_part(origin):
        left = jnp.concatenate(two(x3, origin), axis=1)
        right = wg[0, pl.ds(2 * origin, 2)].reshape(2 * BS, BS)
        return mm(left, right)

    def gd_part(origin):
        left = jnp.concatenate(two(g3, origin), axis=1)
        right = jnp.concatenate((wg[1, 2 * origin], wg[1, 2 * origin + 1]), axis=1)
        return mm_t(left, right)

    for copy in own_w:
        copy.wait()
    pre_ref[...] = pre_part(y)
    gd_ref[...] = gd_part(y)

    def ag_step(w, step):
        for s in range(2):
            for way in range(2):
                if s in ag_slots(step, way):
                    ag_wait(w, step, way, s)
                    if step < NY // 2 and s in ag_slots(step + 1, way):
                        start(ag_copy(w, step + 1, way, s))
        acc, part = ((pre_ref, pre_part), (gd_ref, gd_part))[w]
        if step < NY // 2:
            acc[...] += part(ag_origin(step, 0)) + part(ag_origin(step, 1))
        else:
            acc[...] += part(ag_origin(step, 0))

    for step in range(1, NY // 2 + 1):
        ag_step(0, step)
        if step <= 3:
            pl.semaphore_wait(ready.at[step - 1], 2)
            if step < 3:
                ready_round(step)
        ag_step(1, step)

    keep = keep_ref[...]
    activation, slope = gelu_parts(pre_ref[...])
    dropped = (activation * keep).astype(BF16)
    grad_pre = (gd_ref[...] * keep * slope).astype(BF16)
    gp_ref[...] = grad_pre
    dt_ref[...] = dropped.T
    perm = perm_ref[...]
    ordered = (mm(perm, dropped).astype(BF16), mm(perm, grad_pre).astype(BF16))

    def placed(t, j, lo):
        part = ordered[t][lo:lo + 64]
        if t == 0:
            return mm(part, jnp.concatenate((wg[1, inv[j]], wg[1, inv[j + 1]]), axis=1))
        return mm_t(part, jnp.concatenate((wg[0, inv[j]], wg[0, inv[j + 1]]), axis=0))

    def c_copy(t, h):
        return rdma(c_send.at[t, h], c_recv.at[t, h], c_ss.at[t, h], c_rs.at[t, h], pair_dev)

    for t in range(2):
        for h in range(2):
            for j in range(0, HJ, 2):
                both = placed(t, h * HJ + j, 0).astype(BF16)
                c_send[t, h, j] = both[:, :BS]
                c_send[t, h, j + 1] = both[:, BS:]
            start(c_copy(t, h))

    def term(w, slot):
        if w == 1:
            return mm(dt_ref[...], g3[idxv[slot]])
        return mm(x3t[slot], gp_ref[...])

    def rs_copy(w, step, way, s):
        return rdma(
            rs_send.at[w, way, step - 1, s], rs_recv.at[w, way, step - 1, s],
            rs_ss.at[w, way, step - 1, s], rs_rs.at[w, way, step - 1, s], y_dev[way],
        )

    def rs_piece(w, step, way, s):
        far = NY // 2 + 1 - step
        owner = wrap(y + far if way == 0 else y - far, NY)
        value = term(w, 2 * owner + s)
        if step > 1 and s in rs_slots(step - 1, way):
            rs_copy(w, step - 1, way, s).wait_recv()
            value = value + rs_recv[w, way, step - 2, s].astype(F32)
        rs_send[w, way, step - 1, s] = value.astype(BF16)
        start(rs_copy(w, step, way, s))

    def rs_step(step):
        for w in (1, 0):
            for s in range(2):
                for way in range(2):
                    if s in rs_slots(step, way):
                        rs_piece(w, step, way, s)

    rs_step(1)
    for t in range(2):
        for h in range(2):
            for j in range(0, HJ, 2):
                both = placed(t, h * HJ + j, 64)
                own[t, h, j] = both[:, :BS]
                own[t, h, j + 1] = both[:, BS:]

    X_WAY = (0, 1, 0, 1, 0, 1)
    X_HALF = (0, 1, 1, 0, 0, 1)
    X_CHUNK = (2, 2, 1, 3, 1, 3)

    def x_copy(t, p):
        return rdma(x_send.at[t, p], x_recv.at[t, p], x_ss.at[t, p], x_rs.at[t, p], x_dev[X_WAY[p]])

    def x_own(t, h, chunk):
        span = pl.ds(chunk * 16, 16)
        return own[t, h, :, span, :] + c_recv[t, h, :, span, :].astype(F32)

    for t in range(2):
        for h in range(2):
            c_copy(t, h).wait_recv()
        for p in range(4):
            x_send[t, p] = x_own(t, X_HALF[p], X_CHUNK[p]).astype(BF16)
            start(x_copy(t, p))

    rs_step(2)

    for t in range(2):
        for p in (4, 5):
            x_copy(t, p - 4).wait_recv()
            value = x_own(t, X_HALF[p], X_CHUNK[p]) + x_recv[t, p - 4].astype(F32)
            x_send[t, p] = value.astype(BF16)
            start(x_copy(t, p))

    rs_step(3)

    def z_copy(t, shift):
        return rdma(
            z_send.at[t, shift], z_recv.at[t, shift], z_ss.at[t, shift], z_rs.at[t, shift],
            z_dev(shift),
        )

    for t in range(2):
        for h, (near, far) in enumerate(((3, 4), (2, 5))):
            x_copy(t, near).wait_recv()
            x_copy(t, far).wait_recv()
            value = (
                x_own(t, h, 0) + x_recv[t, near].astype(F32) + x_recv[t, far].astype(F32)
            )
            zsum[t, pl.ds(h * HJ * 16, HJ * 16)] = value.reshape(HJ * 16, BS)
        for shift in Z_ORDER:
            z_send[t, shift] = zsum[t, pl.ds(shift, NJ, stride=16), :].astype(BF16)
            start(z_copy(t, shift))

    rs_step(4)

    for t, o_ref in enumerate((out_ref, ing_ref)):
        total = zsum[t, pl.ds(0, NJ, stride=16), :]
        for shift in Z_ORDER:
            z_copy(t, shift).wait_recv()
            total = total + z_recv[t, shift].astype(F32)
        o_ref[...] = total.astype(BF16)

    for w, o_ref in ((1, gwo_ref), (0, gwi_ref)):
        for s in range(2):
            value = term(w, 2 * y + s)
            for way in range(2):
                rs_copy(w, NY // 2, way, s).wait_recv()
                value = value + rs_recv[w, way, NY // 2 - 1, s].astype(F32)
            o_ref[0, s] = value

    for copy in sends:
        copy.wait_send()


def body(inputs, cotangent, w_in, w_out, block_index, block_count, drop_seeds):
    vmem = pl.BlockSpec(memory_space=pltpu.VMEM)
    smem = pl.BlockSpec(memory_space=pltpu.SMEM)
    anywhere = pl.BlockSpec(memory_space=pl.ANY)
    dma = pltpu.SemaphoreType.DMA
    block = (BS, BS)
    out, ing, gwi, gwo = pl.pallas_call(
        kernel,
        out_shape=(
            jax.ShapeDtypeStruct((NJ, BS), BF16),
            jax.ShapeDtypeStruct((NJ, BS), BF16),
            jax.ShapeDtypeStruct((1, 2, BS, BS), F32),
            jax.ShapeDtypeStruct((1, 2, BS, BS), F32),
        ),
        in_specs=[anywhere] * 4 + [smem] * 2 + [vmem],
        out_specs=(vmem,) * 4,
        scratch_shapes=[
            pltpu.VMEM((NJ + 1, *block), BF16),
            pltpu.VMEM((NJ + 1, *block), BF16),
            pltpu.VMEM((K, *block), BF16),
            pltpu.VMEM((2, K + 1, *block), BF16),
            pltpu.VMEM(block, F32),
            pltpu.VMEM(block, BF16),
            pltpu.VMEM(block, F32),
            pltpu.VMEM(block, F32),
            pltpu.VMEM(block, BF16),
            pltpu.VMEM(block, BF16),
            pltpu.VMEM((2, 2, 4, 2, *block), BF16),
            pltpu.VMEM((2, 2, 4, 2, *block), BF16),
            pltpu.VMEM((2, 2, HJ, 64, BS), BF16),
            pltpu.VMEM((2, 2, HJ, 64, BS), BF16),
            pltpu.VMEM((2, 2, HJ, 64, BS), F32),
            pltpu.VMEM((2, 6, HJ, 16, BS), BF16),
            pltpu.VMEM((2, 6, HJ, 16, BS), BF16),
            pltpu.VMEM((2, NJ * 16, BS), F32),
            pltpu.VMEM((2, NZ, NJ, BS), BF16),
            pltpu.VMEM((2, NZ, NJ, BS), BF16),
            pltpu.SMEM((K,), jnp.int32),
            pltpu.SMEM((NJ,), jnp.int32),
            dma((2, NJ)),
            dma((2,)),
            dma((2, 2, 4, 2)),
            dma((2, 2, 4, 2)),
            dma((2, 2, 4, 2)),
            dma((2, 2, 4, 2)),
            dma((2, 2)),
            dma((2, 2)),
            dma((2, 6)),
            dma((2, 6)),
            dma((2, NZ)),
            dma((2, NZ)),
            pltpu.SemaphoreType.REGULAR((3,)),
        ],
        compiler_params=pltpu.CompilerParams(
            collective_id=0, has_side_effects=True, vmem_limit_bytes=40 << 20
        ),
    )(
        inputs, cotangent, w_in, w_out, block_index, block_count,
        drop_seeds.reshape(1, BS),
    )
    return out.reshape(1, NJ * BS), ing.reshape(1, NJ * BS), gwi, gwo


def solution(mesh):
    placed = (
        P("dp", None),
        P("dp", None),
        P("mp", "dp", None, None),
        P("mp", "dp", None, None),
        P("mp", None),
        P("mp"),
        P("dp"),
    )
    return jax.shard_map(
        body,
        mesh=mesh,
        in_specs=placed,
        out_specs=(
            P(("dp", "mp"), None),
            P(("dp", "mp"), None),
            P("mp", "dp", None, None),
            P("mp", "dp", None, None),
        ),
        check_vma=False,
    )
```

time: 620 us -> 67.5 us (0.11)
  the two profiles are of different devices: /device:TPU:16 before, /device:TPU:8 now
where the time goes in v1:
time: 67.5 us; the launch traced here: 67.1 us
  Pallas kernels  59.4 us (88%)
  local copies, waits for them, and re-layouts  6.44 us (10%)
  between operations  1.31 us (2%)
    pallas_call x1, Pallas kernels, body(): pl.pallas_call(kernel, out_shape=(jax.ShapeDtypeStruct((NJ, BS), BF16), j...  59.4 us
    unnamed x14, local copies, waits for them, and re-layouts  5.82 us

profile of v1, /device:TPU:8, one launch (start us, length us, event | category | flops | bytes accessed | tf_op | source)
XLA Modules:
  0.0 67.1 jit_solution(3451287026756253219)
XLA Ops:
  1.3 0.0 copy-start.4
  1.3 0.0 copy-start.5
  1.3 0.6 copy-done.4
  1.9 0.0 copy-done.5
  2.0 0.0 copy-start
  2.0 1.1 %copy-done = bf16[128,2560]{1,0:T(8,128)(2,1)S(1)} copy-done((bf16[128,2560]{1,0:T(8,128)(2,1)S(1)}, bf16[128,2560]{1,0:T(8,128)(2,1)}, u32[]{:S(2)}) %copy-start) | copy-done | bytes 655384
  3.0 0.0 copy-start.1
  3.0 1.1 %copy-done.1 = bf16[128,2560]{1,0:T(8,128)(2,1)S(1)} copy-done((bf16[128,2560]{1,0:T(8,128)(2,1)S(1)}, bf16[128,2560]{1,0:T(8,128)(2,1)}, u32[]{:S(2)}) %copy-start.1) | copy-done | bytes 655384
  4.1 0.0 copy-start.2
  4.1 0.8 %copy-done.2 = bf16[1,2,128,128]{3,2,1,0:T(8,128)(2,1)S(1)} copy-done((bf16[1,2,128,128]{3,2,1,0:T(8,128)(2,1)S(1)}, bf16[1,2,128,128]{3,2,1,0:T(8,128)(2,1)}, u32[]{:S(2)}) %copy-start.2) | copy-done | bytes 65560
  5.0 0.0 copy-start.3
  5.0 0.8 %copy-done.3 = bf16[1,2,128,128]{3,2,1,0:T(8,128)(2,1)S(1)} copy-done((bf16[1,2,128,128]{3,2,1,0:T(8,128)(2,1)S(1)}, bf16[1,2,128,128]{3,2,1,0:T(8,128)(2,1)}, u32[]{:S(2)}) %copy-start.3) | copy-done | bytes 65560
  5.8 59.4 %shard_map.102 = (bf16[20,128]{1,0:T(8,128)(2,1)S(1)}, bf16[20,128]{1,0:T(8,128)(2,1)S(1)}, f32[1,2,128,128]{3,2,1,0:T(8,128)S(1)}, f32[1,2,128,128]{3,2,1,0:T(8,128)S(1)}) custom-call(bf16[128,2560]{1,0:T(8,128)(2,1)S(1)} %copy-done, bf16[128,2560]{1,0:T(8,128)(2,1)S(1)} %copy-done.1, bf16[1,2,128,128]{3,2,1,0:T(8,128)(2,1)S(1)} %copy-done.2, ...), custom_call_target="tpu_custom_call" | custom-call | tf_op jit(solution)/shard_map/pallas_call | solution.py:353
  65.2 0.6 copy_bitcast_fusion
  65.8 0.7 copy.18
  66.5 0.7 copy.19
Async XLA Ops:
  1.3 0.7 copy-start.4
  1.3 0.7 copy-start.5
  2.0 1.1 %copy-start = (bf16[128,2560]{1,0:T(8,128)(2,1)S(1)}, bf16[128,2560]{1,0:T(8,128)(2,1)}, u32[]{:S(2)}) copy-start(bf16[128,2560]{1,0:T(8,128)(2,1)} %x_hbm.1) | copy-start | bytes 1966084
  3.0 1.1 %copy-start.1 = (bf16[128,2560]{1,0:T(8,128)(2,1)S(1)}, bf16[128,2560]{1,0:T(8,128)(2,1)}, u32[]{:S(2)}) copy-start(bf16[128,2560]{1,0:T(8,128)(2,1)} %g_hbm.1) | copy-start | bytes 1966084
  4.1 0.8 %copy-start.2 = (bf16[1,2,128,128]{3,2,1,0:T(8,128)(2,1)S(1)}, bf16[1,2,128,128]{3,2,1,0:T(8,128)(2,1)}, u32[]{:S(2)}) copy-start(bf16[1,2,128,128]{3,2,1,0:T(8,128)(2,1)} %wi_hbm.1) | copy-start | bytes 196612
  5.0 0.8 %copy-start.3 = (bf16[1,2,128,128]{3,2,1,0:T(8,128)(2,1)S(1)}, bf16[1,2,128,128]{3,2,1,0:T(8,128)(2,1)}, u32[]{:S(2)}) copy-start(bf16[1,2,128,128]{3,2,1,0:T(8,128)(2,1)} %wo_hbm.1) | copy-start | bytes 196612

commit v2 on v1

--- a/solution.py
+++ b/solution.py
@@ -1,3 +1,4 @@
+import contextlib
 import math
 
 import jax
@@ -20,6 +21,10 @@
 Z_ORDER = (8, 7, 9, 6, 10, 5, 11, 4, 12, 3, 13, 2, 14, 1, 15)
 
 
+def phase(name):
+    return contextlib.nullcontext(name)
+
+
 def scramble(value):
     for _ in range(2):
         value = value ^ lax.shift_right_logical(value, jnp.int32(16))
@@ -63,12 +68,12 @@
 
 
 def kernel(
-    x_hbm, g_hbm, wi_hbm, wo_hbm, idx_ref, cnt_ref, seed_ref,
+    x_hbm, g_hbm, wi_hbm, wo_hbm, idx_hbm, cnt_hbm, seed_hbm,
     out_ref, ing_ref, gwi_ref, gwo_ref,
     x3, g3, x3t, wg, keep_ref, perm_ref, pre_ref, gd_ref, dt_ref, gp_ref,
     rs_send, rs_recv, c_send, c_recv, own, x_send, x_recv, zsum, z_send, z_recv,
-    idxv, inv,
-    ld_sem, wl_sem, ag_ss, ag_rs, rs_ss, rs_rs, c_ss, c_rs, x_ss, x_rs, z_ss, z_rs, ready,
+    idx_ref, cnt_ref, seed_ref, idxv, inv,
+    sm_sem, ld_sem, wl_sem, ag_ss, ag_rs, rs_ss, rs_rs, c_ss, c_rs, x_ss, x_rs, z_ss, z_rs, ready,
 ):
     y = lax.axis_index("dp")
     mp = lax.axis_index("mp")
@@ -105,9 +110,16 @@
     around = (*y_dev, *x_dev, z_dev(1), z_dev(-1), pair_dev)
     for device in around:
         pl.semaphore_signal(barrier, inc=1, device_id=device, device_id_type=MESH)
-    for copy in own_w + loads:
+    small = [
+        pltpu.make_async_copy(src, dst, sm_sem.at[i])
+        for i, (src, dst) in enumerate(
+            ((idx_hbm, idx_ref), (seed_hbm, seed_ref))
+        )
+    ]
+    for copy in small + own_w + loads:
         copy.start()
-    pl.semaphore_wait(barrier, len(around))
+    with phase("barrier"):
+        pl.semaphore_wait(barrier, len(around))
 
     def ag_origin(step, way):
         return wrap(y - step if way == 0 else y + step, NY)
@@ -137,8 +149,10 @@
             for way in range(2):
                 start(ag_copy(w, 1, way, s))
 
+    for copy in small:
+        copy.wait()
     for k in range(K):
-        idxv[k] = jnp.where(k < cnt_ref[0], idx_ref[0, k], NJ)
+        idxv[k] = jnp.where(k < cnt_hbm[0], idx_ref[0, k], NJ)
     for j in range(NJ):
         found = jnp.int32(K)
         for k in range(K):
@@ -162,8 +176,9 @@
     token = tok_x * 32 + tok_z * 2 + tok_c
     perm_ref[...] = jnp.where(token == cols, F32(1.0), F32(0.0)).astype(BF16)
 
-    for copy in loads:
-        copy.wait()
+    with phase("loads"):
+        for copy in loads:
+            copy.wait()
 
     def ready_round(r):
         for shift in (1 << r, -(1 << r)):
@@ -188,10 +203,11 @@
         right = jnp.concatenate((wg[1, 2 * origin], wg[1, 2 * origin + 1]), axis=1)
         return mm_t(left, right)
 
-    for copy in own_w:
-        copy.wait()
-    pre_ref[...] = pre_part(y)
-    gd_ref[...] = gd_part(y)
+    with phase("own_slots"):
+        for copy in own_w:
+            copy.wait()
+        pre_ref[...] = pre_part(y)
+        gd_ref[...] = gd_part(y)
 
     def ag_step(w, step):
         for s in range(2):
@@ -207,21 +223,25 @@
             acc[...] += part(ag_origin(step, 0))
 
     for step in range(1, NY // 2 + 1):
-        ag_step(0, step)
+        with phase(f"gather_in_{step}"):
+            ag_step(0, step)
         if step <= 3:
-            pl.semaphore_wait(ready.at[step - 1], 2)
+            with phase(f"ready_{step}"):
+                pl.semaphore_wait(ready.at[step - 1], 2)
             if step < 3:
                 ready_round(step)
-        ag_step(1, step)
-
-    keep = keep_ref[...]
-    activation, slope = gelu_parts(pre_ref[...])
-    dropped = (activation * keep).astype(BF16)
-    grad_pre = (gd_ref[...] * keep * slope).astype(BF16)
-    gp_ref[...] = grad_pre
-    dt_ref[...] = dropped.T
-    perm = perm_ref[...]
-    ordered = (mm(perm, dropped).astype(BF16), mm(perm, grad_pre).astype(BF16))
+        with phase(f"gather_out_{step}"):
+            ag_step(1, step)
+
+    with phase("gelu"):
+        keep = keep_ref[...]
+        activation, slope = gelu_parts(pre_ref[...])
+        dropped = (activation * keep).astype(BF16)
+        grad_pre = (gd_ref[...] * keep * slope).astype(BF16)
+        gp_ref[...] = grad_pre
+        dt_ref[...] = dropped.T
+        perm = perm_ref[...]
+        ordered = (mm(perm, dropped).astype(BF16), mm(perm, grad_pre).astype(BF16))
 
     def placed(t, j, lo):
         part = ordered[t][lo:lo + 64]
@@ -232,13 +252,14 @@
     def c_copy(t, h):
         return rdma(c_send.at[t, h], c_recv.at[t, h], c_ss.at[t, h], c_rs.at[t, h], pair_dev)
 
-    for t in range(2):
-        for h in range(2):
-            for j in range(0, HJ, 2):
-                both = placed(t, h * HJ + j, 0).astype(BF16)
-                c_send[t, h, j] = both[:, :BS]
-                c_send[t, h, j + 1] = both[:, BS:]
-            start(c_copy(t, h))
+    with phase("pair_half"):
+        for t in range(2):
+            for h in range(2):
+                for j in range(0, HJ, 2):
+                    both = placed(t, h * HJ + j, 0).astype(BF16)
+                    c_send[t, h, j] = both[:, :BS]
+                    c_send[t, h, j + 1] = both[:, BS:]
+                start(c_copy(t, h))
 
     def term(w, slot):
         if w == 1:
@@ -268,13 +289,15 @@
                     if s in rs_slots(step, way):
                         rs_piece(w, step, way, s)
 
-    rs_step(1)
-    for t in range(2):
-        for h in range(2):
-            for j in range(0, HJ, 2):
-                both = placed(t, h * HJ + j, 64)
-                own[t, h, j] = both[:, :BS]
-                own[t, h, j + 1] = both[:, BS:]
+    with phase("reduce_1"):
+        rs_step(1)
+    with phase("own_half"):
+        for t in range(2):
+            for h in range(2):
+                for j in range(0, HJ, 2):
+                    both = placed(t, h * HJ + j, 64)
+                    own[t, h, j] = both[:, :BS]
+                    own[t, h, j + 1] = both[:, BS:]
 
     X_WAY = (0, 1, 0, 1, 0, 1)
     X_HALF = (0, 1, 1, 0, 0, 1)
@@ -288,22 +311,26 @@
         return own[t, h, :, span, :] + c_recv[t, h, :, span, :].astype(F32)
 
     for t in range(2):
-        for h in range(2):
-            c_copy(t, h).wait_recv()
+        with phase(f"pair_wait_{t}"):
+            for h in range(2):
+                c_copy(t, h).wait_recv()
         for p in range(4):
             x_send[t, p] = x_own(t, X_HALF[p], X_CHUNK[p]).astype(BF16)
             start(x_copy(t, p))
 
-    rs_step(2)
+    with phase("reduce_2"):
+        rs_step(2)
 
     for t in range(2):
         for p in (4, 5):
-            x_copy(t, p - 4).wait_recv()
+            with phase(f"x_first_{t}_{p}"):
+                x_copy(t, p - 4).wait_recv()
             value = x_own(t, X_HALF[p], X_CHUNK[p]) + x_recv[t, p - 4].astype(F32)
             x_send[t, p] = value.astype(BF16)
             start(x_copy(t, p))
 
-    rs_step(3)
+    with phase("reduce_3"):
+        rs_step(3)
 
     def z_copy(t, shift):
         return rdma(
@@ -313,8 +340,9 @@
 
     for t in range(2):
         for h, (near, far) in enumerate(((3, 4), (2, 5))):
-            x_copy(t, near).wait_recv()
-            x_copy(t, far).wait_recv()
+            with phase(f"x_second_{t}_{h}"):
+                x_copy(t, near).wait_recv()
+                x_copy(t, far).wait_recv()
             value = (
                 x_own(t, h, 0) + x_recv[t, near].astype(F32) + x_recv[t, far].astype(F32)
             )
@@ -323,42 +351,59 @@
             z_send[t, shift] = zsum[t, pl.ds(shift, NJ, stride=16), :].astype(BF16)
             start(z_copy(t, shift))
 
-    rs_step(4)
+    with phase("reduce_4"):
+        rs_step(4)
 
     for t, o_ref in enumerate((out_ref, ing_ref)):
         total = zsum[t, pl.ds(0, NJ, stride=16), :]
         for shift in Z_ORDER:
-            z_copy(t, shift).wait_recv()
+            with phase(f"z_{t}_{shift}"):
+                z_copy(t, shift).wait_recv()
             total = total + z_recv[t, shift].astype(F32)
-        o_ref[...] = total.astype(BF16)
+        for j in range(NJ):
+            o_ref[:, j * BS:(j + 1) * BS] = total[j:j + 1].astype(BF16)
 
     for w, o_ref in ((1, gwo_ref), (0, gwi_ref)):
         for s in range(2):
             value = term(w, 2 * y + s)
             for way in range(2):
-                rs_copy(w, NY // 2, way, s).wait_recv()
+                with phase(f"reduce_end_{w}_{s}_{way}"):
+                    rs_copy(w, NY // 2, way, s).wait_recv()
                 value = value + rs_recv[w, way, NY // 2 - 1, s].astype(F32)
             o_ref[0, s] = value
 
-    for copy in sends:
-        copy.wait_send()
+    with phase("sent"):
+        for copy in sends:
+            copy.wait_send()
+
+
+def put_out(*refs):
+    copies = [
+        pltpu.make_async_copy(refs[i], refs[4 + i], refs[8].at[i]) for i in range(4)
+    ]
+    for copy in copies:
+        copy.start()
+    for copy in copies:
+        copy.wait()
 
 
 def body(inputs, cotangent, w_in, w_out, block_index, block_count, drop_seeds):
     vmem = pl.BlockSpec(memory_space=pltpu.VMEM)
-    smem = pl.BlockSpec(memory_space=pltpu.SMEM)
-    anywhere = pl.BlockSpec(memory_space=pl.ANY)
+    hbm = pl.BlockSpec(memory_space=pltpu.HBM)
     dma = pltpu.SemaphoreType.DMA
     block = (BS, BS)
-    out, ing, gwi, gwo = pl.pallas_call(
+    results = (
+        jax.ShapeDtypeStruct((1, NJ * BS), BF16),
+        jax.ShapeDtypeStruct((1, NJ * BS), BF16),
+        jax.ShapeDtypeStruct((1, 2, BS, BS), F32),
+        jax.ShapeDtypeStruct((1, 2, BS, BS), F32),
+    )
+    held = pl.pallas_call(
         kernel,
         out_shape=(
-            jax.ShapeDtypeStruct((NJ, BS), BF16),
-            jax.ShapeDtypeStruct((NJ, BS), BF16),
-            jax.ShapeDtypeStruct((1, 2, BS, BS), F32),
-            jax.ShapeDtypeStruct((1, 2, BS, BS), F32),
+            *results,
         ),
-        in_specs=[anywhere] * 4 + [smem] * 2 + [vmem],
+        in_specs=[hbm] * 5 + [pl.BlockSpec(memory_space=pltpu.SMEM), hbm],
         out_specs=(vmem,) * 4,
         scratch_shapes=[
             pltpu.VMEM((NJ + 1, *block), BF16),
@@ -381,8 +426,12 @@
             pltpu.VMEM((2, NJ * 16, BS), F32),
             pltpu.VMEM((2, NZ, NJ, BS), BF16),
             pltpu.VMEM((2, NZ, NJ, BS), BF16),
+            pltpu.SMEM((1, K), jnp.int32),
+            pltpu.SMEM((1,), jnp.int32),
+            pltpu.VMEM((1, BS), jnp.int32),
             pltpu.SMEM((K,), jnp.int32),
             pltpu.SMEM((NJ,), jnp.int32),
+            dma((3,)),
             dma((2, NJ)),
             dma((2,)),
             dma((2, 2, 4, 2)),
@@ -401,10 +450,21 @@
             collective_id=0, has_side_effects=True, vmem_limit_bytes=40 << 20
         ),
     )(
-        inputs, cotangent, w_in, w_out, block_index, block_count,
-        drop_seeds.reshape(1, BS),
-    )
-    return out.reshape(1, NJ * BS), ing.reshape(1, NJ * BS), gwi, gwo
+        *(
+            pltpu.with_memory_space_constraint(value, pltpu.HBM)
+            for value in (
+                inputs, cotangent, w_in, w_out, block_index
+            )
+        ), block_count, pltpu.with_memory_space_constraint(drop_seeds.reshape(1, BS), pltpu.HBM)
+    )
+    return pl.pallas_call(
+        put_out,
+        out_shape=results,
+        in_specs=[vmem] * 4,
+        out_specs=(hbm,) * 4,
+        scratch_shapes=[dma((4,))],
+        compiler_params=pltpu.CompilerParams(vmem_limit_bytes=1 << 20),
+    )(*held)
 
 
 def solution(mesh):

time: 67.5 us -> 61.3 us (0.908)
  local copies, waits for them, and re-layouts: 6.44 us -> 0 us
    unnamed x14 -> x0, local copies, waits for them, and re-layouts: 5.82 us -> none
    pallas_call x1 -> x2, Pallas kernels: 59.4 us -> 59.9 us  [the longest x1 59.1 us: body(): pl.pallas_call(kernel, out_shape=(*results,), in_specs=[hbm] * 5 + [pl.Bl...]
where the time goes in v2:
time: 61.3 us; the launch traced here: 61.1 us
  Pallas kernels  59.9 us (98%)
  between operations  1.29 us (2%)
    pallas_call x1, Pallas kernels, body(): pl.pallas_call(kernel, out_shape=(*results,), in_specs=[hbm] * 5 + [pl.Bl...  59.1 us

profile of v2, /device:TPU:8, one launch (start us, length us, event | category | flops | bytes accessed | tf_op | source)
XLA Modules:
  0.0 61.1 jit_solution(14866214054488245081)
XLA Ops:
  1.3 59.1 %shard_map.102 = (bf16[1,2560]{1,0:T(2,128)(2,1)S(1)}, bf16[1,2560]{1,0:T(2,128)(2,1)S(1)}, f32[1,2,128,128]{3,2,1,0:T(8,128)S(1)}, f32[1,2,128,128]{3,2,1,0:T(8,128)S(1)}) custom-call(bf16[128,2560]{1,0:T(8,128)(2,1)} %x_hbm.1, bf16[128,2560]{1,0:T(8,128)(2,1)} %g_hbm.1, bf16[1,2,128,128]{3,2,1,0:T(8,128)(2,1)} %wi_hbm.1, bf16[1,2,128,128]{3,2,1,0:T(8,128)(2,1)} %wo_hbm.1, ...), custom_call_target="tpu_custom_call" | custom-call | tf_op jit(solution)/shard_map/pallas_call | solution.py:401
  60.4 0.7 %shard_map.103 = (bf16[1,2560]{1,0:T(2,128)(2,1)}, bf16[1,2560]{1,0:T(2,128)(2,1)}, f32[1,2,128,128]{3,2,1,0:T(8,128)}, f32[1,2,128,128]{3,2,1,0:T(8,128)}) custom-call(bf16[1,2560]{1,0:T(2,128)(2,1)S(1)} %get-tuple-element.8.refs_0_, bf16[1,2560]{1,0:T(2,128)(2,1)S(1)} %get-tuple-element.9.refs_1_, f32[1,2,128,128]{3,2,1,0:T(8,128)S(1)} %get-tuple-element.10.refs_2_, ...), custom_call_target="tpu_custom_call" | custom-call | tf_op jit(solution)/shard_map/pallas_call | solution.py:460

commit v3 on v2

v3 whole, which is shorter than its diff:
```python
import math

import jax
import jax.numpy as jnp
from jax import lax
from jax.experimental import pallas as pl
from jax.experimental.pallas import tpu as pltpu
from jax.sharding import PartitionSpec as P

BS = 128
K = 16
NJ = 20
GROUP = 8
HALF = GROUP // 2
NG = 2 * NJ // GROUP
NY = 8
NX = 4
NZ = 16
MESH = pl.DeviceIdType.MESH
F32 = jnp.float32
BF16 = jnp.bfloat16
Z_ORDER = (8, 7, 9, 6, 10, 5, 11, 4, 12, 3, 13, 2, 14, 1, 15)


def scramble(value):
    for _ in range(2):
        value = value ^ lax.shift_right_logical(value, jnp.int32(16))
        value = value * jnp.int32(73244475)
    return value ^ lax.shift_right_logical(value, jnp.int32(16))


def gelu_parts(pre_act):
    coeff = math.sqrt(2.0 / math.pi)
    square = pre_act * pre_act
    inner = coeff * (pre_act + 0.044715 * (square * pre_act))
    tanh_val = jnp.tanh(inner)
    activation = 0.5 * pre_act * (1.0 + tanh_val)
    slope = 0.5 * (1.0 + tanh_val) + 0.5 * pre_act * (1.0 - tanh_val * tanh_val) * coeff * (
        1.0 + 3.0 * 0.044715 * square
    )
    return activation, slope


def mm(a, b):
    return lax.dot_general(a, b, (((1,), (0,)), ((), ())), preferred_element_type=F32)


def mm_t(a, b):
    return lax.dot_general(a, b, (((1,), (1,)), ((), ())), preferred_element_type=F32)


def rdma(src, dst, send_sem, recv_sem, device):
    return pltpu.make_async_remote_copy(
        src_ref=src, dst_ref=dst, send_sem=send_sem, recv_sem=recv_sem,
        device_id=device, device_id_type=MESH,
    )


def ag_slots(step, way):
    return (0, 1) if step < NY // 2 else (way,)


def rs_slots(step, way):
    return (0, 1) if step > 1 else (way,)


RS_FLAT = {
    key: i
    for i, key in enumerate(
        (step, way, s) for step in range(1, 5) for way in range(2) for s in rs_slots(step, way)
    )
}
X_WAY = (0, 1, 0, 1, 0, 1)
X_SUB = (0, 1, 1, 0, 0, 1)
X_CHUNK = (2, 2, 1, 3, 1, 3)


def kernel(
    x_hbm, g_hbm, wi_hbm, wo_hbm, idx_hbm, cnt_ref, seed_hbm,
    out_ref, ing_ref, gwi_ref, gwo_ref,
    x3, g3, x3t, wg, keep_ref, perm_ref, pre_ref, gd_ref, dt_ref, gp_ref,
    rs_send, rs_recv, c_send, c_recv, own, x_send, x_recv, zsum, z_send, z_recv,
    idx_ref, seed_ref, idxv, inv,
    sm_sem, ld_sem, wl_sem, ag_ss, ag_rs, rs_ss, rs_rs, c_ss, c_rs, x_ss, x_rs, z_ss, z_rs, ready,
):
    y = lax.axis_index("dp")
    mp = lax.axis_index("mp")
    core = lax.rem(mp, 2)
    z = lax.rem(lax.div(mp, 2), NZ)
    x = lax.div(mp, 2 * NZ)

    def at(yy, xx, zz, cc):
        return (yy, (xx * NZ + zz) * 2 + cc)

    def wrap(value, size):
        return lax.rem(value + size, size)

    y_dev = (at(wrap(y + 1, NY), x, z, core), at(wrap(y - 1, NY), x, z, core))
    x_dev = (at(y, wrap(x + 1, NX), z, core), at(y, wrap(x - 1, NX), z, core))
    pair_dev = at(y, x, z, 1 - core)

    def z_dev(shift):
        return at(y, x, wrap(z + shift, NZ), core)

    w_hbm = (wi_hbm, wo_hbm)

    barrier = pltpu.get_barrier_semaphore()
    around = (*y_dev, *x_dev, z_dev(1), z_dev(-1), pair_dev)
    for device in around:
        pl.semaphore_signal(barrier, inc=1, device_id=device, device_id_type=MESH)

    small = [
        pltpu.make_async_copy(idx_hbm, idx_ref, sm_sem.at[0]),
        pltpu.make_async_copy(seed_hbm, seed_ref, sm_sem.at[1]),
    ]
    own_w = [
        pltpu.make_async_copy(w_hbm[w].at[0], wg.at[w, pl.ds(2 * y, 2)], wl_sem.at[w])
        for w in range(2)
    ]
    for copy in small + own_w:
        copy.start()
    for j in range(NJ):
        cols = pl.ds(j * BS, BS)
        pltpu.make_async_copy(x_hbm.at[:, cols], x3.at[j], ld_sem.at[0]).start()
        pltpu.make_async_copy(g_hbm.at[:, cols], g3.at[j], ld_sem.at[1]).start()
    pl.semaphore_wait(barrier, len(around))

    def ag_origin(step, way):
        return wrap(y - step if way == 0 else y + step, NY)

    def ag_copy(w, step, way, s):
        slot = 2 * ag_origin(step - 1, way) + s
        src = w_hbm[w].at[0, s] if step == 1 else wg.at[w, slot]
        return rdma(
            src, wg.at[w, slot], ag_ss.at[w], ag_rs.at[w, way, step - 1, s], y_dev[way]
        )

    def ag_wait(w, step, way, s):
        here = wg.at[w, 2 * ag_origin(step, way) + s]
        rdma(
            here, here, ag_ss.at[w], ag_rs.at[w, way, step - 1, s], y_dev[way]
        ).wait_recv()

    for w in range(2):
        for s in range(2):
            for way in range(2):
                ag_copy(w, 1, way, s).start()

    for copy in small:
        copy.wait()
    for k in range(K):
        idxv[k] = jnp.where(k < cnt_ref[0], idx_ref[0, k], NJ)
    for j in range(NJ):
        found = jnp.int32(K)
        for k in range(K):
            found = jnp.where(idxv[k] == j, k, found)
        inv[j] = found
    blank = jnp.zeros((BS, BS), BF16)
    x3[NJ] = blank
    g3[NJ] = blank
    wg[0, K] = blank
    wg[1, K] = blank

    rows = lax.broadcasted_iota(jnp.int32, (BS, BS), 0)
    cols = lax.broadcasted_iota(jnp.int32, (BS, BS), 1)
    seeds = jnp.broadcast_to(seed_ref[...], (BS, BS)).T
    mixed = scramble(seeds + (mp * BS + cols) * jnp.int32(668265261))
    keep_ref[...] = jnp.where((mixed & 7) != 0, F32(8.0 / 7.0), F32(0.0))
    half = lax.shift_right_logical(rows, 6)
    tok_x = (x + (lax.shift_right_logical(rows, 4) & 3)) & 3
    tok_z = (z + (rows & 15)) & 15
    tok_c = jnp.where(half == 1, core, 1 - core)
    token = tok_x * 32 + tok_z * 2 + tok_c
    perm_ref[...] = jnp.where(token == cols, F32(1.0), F32(0.0)).astype(BF16)

    for i, ref in enumerate((x3, g3)):
        whole = ref.at[pl.ds(0, NJ)]
        pltpu.make_async_copy(whole, whole, ld_sem.at[i]).wait()

    def ready_round(r):
        for shift in (1 << r, -(1 << r)):
            pl.semaphore_signal(
                ready.at[r], inc=1, device_id=z_dev(shift), device_id_type=MESH
            )

    ready_round(0)

    def two(ref, origin):
        return ref[idxv[2 * origin]], ref[idxv[2 * origin + 1]]

    def pre_part(origin):
        left = jnp.concatenate(two(x3, origin), axis=1)
        right = wg[0, pl.ds(2 * origin, 2)].reshape(2 * BS, BS)
        return mm(left, right)

    def gd_part(origin):
        left = jnp.concatenate(two(g3, origin), axis=1)
        right = jnp.concatenate((wg[1, 2 * origin], wg[1, 2 * origin + 1]), axis=1)
        return mm_t(left, right)

    for copy in own_w:
        copy.wait()

    def ag_step(w, step):
        for s in range(2):
            for way in range(2):
                if s in ag_slots(step, way):
                    ag_wait(w, step, way, s)
                    if step < NY // 2 and s in ag_slots(step + 1, way):
                        ag_copy(w, step + 1, way, s).start()

    pre_ref[...] = pre_part(y)
    gd_ref[...] = gd_part(y)
    for step in range(1, NY // 2):
        ag_step(0, step)
        ag_step(1, step)
        pl.semaphore_wait(ready.at[step - 1], 2)
        if step < 3:
            ready_round(step)
        if step == 1:
            for k in range(K):
                x3t[k] = x3[idxv[k]].T
        left, right = ag_origin(step, 0), ag_origin(step, 1)
        pre_ref[...] += pre_part(left) + pre_part(right)
        gd_ref[...] += gd_part(left) + gd_part(right)

    perm = perm_ref[...]
    keep = keep_ref[...]
    far = ag_origin(NY // 2, 0)
    ag_step(0, NY // 2)
    activation, slope = gelu_parts(pre_ref[...] + pre_part(far))
    dropped = (activation * keep).astype(BF16)
    slope = slope * keep
    dt_ref[...] = dropped.T
    first = mm(perm, dropped).astype(BF16)
    ag_step(1, NY // 2)
    grad_pre = ((gd_ref[...] + gd_part(far)) * slope).astype(BF16)
    gp_ref[...] = grad_pre
    ordered = (first, mm(perm, grad_pre).astype(BF16))

    def placed(u, lo):
        t, j = divmod(u, NJ)
        part = ordered[t][lo:lo + 64]
        if t == 0:
            return mm(part, jnp.concatenate((wg[1, inv[j]], wg[1, inv[j + 1]]), axis=1))
        return mm_t(part, jnp.concatenate((wg[0, inv[j]], wg[0, inv[j + 1]]), axis=0))

    def fill(ref, g, lo):
        for i in range(0, GROUP, 2):
            both = placed(g * GROUP + i, lo).astype(ref.dtype)
            ref[g, i] = both[:, :BS]
            ref[g, i + 1] = both[:, BS:]

    def c_copy(g):
        return rdma(c_send.at[g], c_recv.at[g], c_ss, c_rs.at[g], pair_dev)

    def pair_out(g):
        fill(c_send, g, 0)
        c_copy(g).start()

    def term(w, slot):
        if w == 1:
            return mm(dt_ref[...], g3[idxv[slot]])
        return mm(x3t[slot], gp_ref[...])

    def rs_copy(w, step, way, s):
        i = RS_FLAT[step, way, s]
        return rdma(rs_send.at[w, i], rs_recv.at[w, i], rs_ss.at[w], rs_rs.at[w, i], y_dev[way])

    def rs_piece(w, step, way, s):
        far = NY // 2 + 1 - step
        owner = wrap(y + far if way == 0 else y - far, NY)
        value = term(w, 2 * owner + s)
        if step > 1 and s in rs_slots(step - 1, way):
            rs_copy(w, step - 1, way, s).wait_recv()
            value = value + rs_recv[w, RS_FLAT[step - 1, way, s]].astype(F32)
        rs_send[w, RS_FLAT[step, way, s]] = value.astype(BF16)
        rs_copy(w, step, way, s).start()

    def rs_both(w, step, chain):
        for way in range(2):
            rs_piece(w, step, way, way ^ chain)

    def rs_end(w, s):
        value = term(w, 2 * y + s)
        for way in range(2):
            rs_copy(w, NY // 2, way, s).wait_recv()
            value = value + rs_recv[w, RS_FLAT[NY // 2, way, s]].astype(F32)
        (gwi_ref, gwo_ref)[w][0, s] = value

    def x_copy(g, p):
        sem = x_rs.at[g, min(p, 2)]
        return rdma(x_send.at[g, p], x_recv.at[g, p], x_ss, sem, x_dev[X_WAY[p]])

    def x_own(g, sub, chunk):
        some, span = pl.ds(sub * HALF, HALF), pl.ds(chunk * 16, 16)
        return own[g, some, span, :] + c_recv[g, some, span, :].astype(F32)

    def x_first(g):
        c_copy(g).wait_recv()
        for p in range(4):
            x_send[g, p] = x_own(g, X_SUB[p], X_CHUNK[p]).astype(BF16)
            x_copy(g, p).start()

    def x_second(g):
        for p in (4, 5):
            x_copy(g, p - 4).wait_recv()
            value = x_own(g, X_SUB[p], X_CHUNK[p]) + x_recv[g, p - 4].astype(F32)
            x_send[g, p] = value.astype(BF16)
            x_copy(g, p).start()

    def z_first(g):
        last = pl.ds(2, 4)
        rdma(x_send.at[g, last], x_recv.at[g, last], x_ss, x_rs.at[g, 2], x_dev[0]).wait_recv()
        for sub, (near, more) in enumerate(((3, 4), (2, 5))):
            value = x_own(g, sub, 0) + x_recv[g, near].astype(F32) + x_recv[g, more].astype(F32)
            zsum[g, pl.ds(sub * HALF * NZ, HALF * NZ)] = value.reshape(HALF * NZ, BS)
        for shift in Z_ORDER:
            z_send[g, shift] = zsum[g, pl.ds(shift, GROUP, stride=NZ), :].astype(BF16)
            rdma(
                z_send.at[g, shift], z_recv.at[g, shift], z_ss, z_rs.at[g], z_dev(shift)
            ).start()

    others = pl.ds(1, NZ - 1)

    def z_end(g):
        rdma(
            z_send.at[g, others], z_recv.at[g, others], z_ss, z_rs.at[g], z_dev(1)
        ).wait_recv()
        total = zsum[g, pl.ds(0, GROUP, stride=NZ), :]
        for shift in Z_ORDER:
            total = total + z_recv[g, shift].astype(F32)
        for i in range(GROUP):
            t, j = divmod(g * GROUP + i, NJ)
            (out_ref, ing_ref)[t][:, j * BS:(j + 1) * BS] = total[i:i + 1].astype(BF16)

    pair_out(0)
    for w in (1, 0):
        rs_both(w, 1, 0)
    pair_out(1)
    for w in (1, 0):
        rs_both(w, 2, 1)
    for g in range(2, NG):
        pair_out(g)
    for g in range(NG):
        fill(own, g, 64)
    x_first(0)
    x_first(1)
    rs_both(1, 2, 0)
    x_first(2)
    rs_both(0, 2, 0)
    x_second(0)
    x_first(3)
    rs_both(1, 3, 1)
    x_second(1)
    x_first(4)
    rs_both(0, 3, 1)
    x_second(2)
    rs_both(1, 3, 0)
    z_first(0)
    rs_both(0, 3, 0)
    x_second(3)
    z_first(1)
    rs_both(1, 4, 1)
    x_second(4)
    z_first(2)
    rs_both(0, 4, 1)
    rs_both(1, 4, 0)
    z_first(3)
    rs_both(0, 4, 0)
    z_first(4)
    for w in (1, 0):
        rs_end(w, 0)
        rs_end(w, 1)
    for g in range(NG):
        z_end(g)

    for w in range(2):
        here = wg.at[w, pl.ds(0, 14)]
        rdma(here, here, ag_ss.at[w], ag_rs.at[w, 0, 0, 0], y_dev[0]).wait_send()
        rdma(rs_send.at[w], rs_recv.at[w], rs_ss.at[w], rs_rs.at[w, 0], y_dev[0]).wait_send()
    rdma(c_send, c_recv, c_ss, c_rs.at[0], pair_dev).wait_send()
    rdma(x_send, x_recv, x_ss, x_rs.at[0, 0], x_dev[0]).wait_send()
    rdma(
        z_send.at[:, others], z_recv.at[:, others], z_ss, z_rs.at[0], z_dev(1)
    ).wait_send()


def put_out(*refs):
    copies = [
        pltpu.make_async_copy(refs[i], refs[4 + i], refs[8].at[i]) for i in range(4)
    ]
    for copy in copies:
        copy.start()
    for copy in copies:
        copy.wait()


def body(inputs, cotangent, w_in, w_out, block_index, block_count, drop_seeds):
    vmem = pl.BlockSpec(memory_space=pltpu.VMEM)
    hbm = pl.BlockSpec(memory_space=pltpu.HBM)
    dma = pltpu.SemaphoreType.DMA
    block = (BS, BS)
    results = (
        jax.ShapeDtypeStruct((1, NJ * BS), BF16),
        jax.ShapeDtypeStruct((1, NJ * BS), BF16),
        jax.ShapeDtypeStruct((1, 2, BS, BS), F32),
        jax.ShapeDtypeStruct((1, 2, BS, BS), F32),
    )
    held = pl.pallas_call(
        kernel,
        out_shape=(
            *results,
        ),
        in_specs=[hbm] * 5 + [pl.BlockSpec(memory_space=pltpu.SMEM), hbm],
        out_specs=(vmem,) * 4,
        scratch_shapes=[
            pltpu.VMEM((NJ + 1, *block), BF16),
            pltpu.VMEM((NJ + 1, *block), BF16),
            pltpu.VMEM((K, *block), BF16),
            pltpu.VMEM((2, K + 1, *block), BF16),
            pltpu.VMEM(block, F32),
            pltpu.VMEM(block, BF16),
            pltpu.VMEM(block, F32),
            pltpu.VMEM(block, F32),
            pltpu.VMEM(block, BF16),
            pltpu.VMEM(block, BF16),
            pltpu.VMEM((2, 14, *block), BF16),
            pltpu.VMEM((2, 14, *block), BF16),
            pltpu.VMEM((NG, GROUP, 64, BS), BF16),
            pltpu.VMEM((NG, GROUP, 64, BS), BF16),
            pltpu.VMEM((NG, GROUP, 64, BS), F32),
            pltpu.VMEM((NG, 6, HALF, 16, BS), BF16),
            pltpu.VMEM((NG, 6, HALF, 16, BS), BF16),
            pltpu.VMEM((NG, GROUP * NZ, BS), F32),
            pltpu.VMEM((NG, NZ, GROUP, BS), BF16),
            pltpu.VMEM((NG, NZ, GROUP, BS), BF16),
            pltpu.SMEM((1, K), jnp.int32),
            pltpu.VMEM((1, BS), jnp.int32),
            pltpu.SMEM((K,), jnp.int32),
            pltpu.SMEM((NJ,), jnp.int32),
            dma((2,)),
            dma((2,)),
            dma((2,)),
            dma((2,)),
            dma((2, 2, 4, 2)),
            dma((2,)),
            dma((2, 14)),
            dma(()),
            dma((NG,)),
            dma(()),
            dma((NG, 3)),
            dma(()),
            dma((NG,)),
            pltpu.SemaphoreType.REGULAR((3,)),
        ],
        compiler_params=pltpu.CompilerParams(
            collective_id=0, has_side_effects=True, vmem_limit_bytes=40 << 20
        ),
    )(
        *(
            pltpu.with_memory_space_constraint(value, pltpu.HBM)
            for value in (
                inputs, cotangent, w_in, w_out, block_index
            )
        ), block_count, pltpu.with_memory_space_constraint(drop_seeds.reshape(1, BS), pltpu.HBM)
    )
    return pl.pallas_call(
        put_out,
        out_shape=results,
        in_specs=[vmem] * 4,
        out_specs=(hbm,) * 4,
        scratch_shapes=[dma((4,))],
        compiler_params=pltpu.CompilerParams(vmem_limit_bytes=1 << 20),
    )(*held)


def solution(mesh):
    placed = (
        P("dp", None),
        P("dp", None),
        P("mp", "dp", None, None),
        P("mp", "dp", None, None),
        P("mp", None),
        P("mp"),
        P("dp"),
    )
    return jax.shard_map(
        body,
        mesh=mesh,
        in_specs=placed,
        out_specs=(
            P(("dp", "mp"), None),
            P(("dp", "mp"), None),
            P("mp", "dp", None, None),
            P("mp", "dp", None, None),
        ),
        check_vma=False,
    )
```

time: 61.3 us -> 58.6 us (0.956)
  Pallas kernels: 59.9 us -> 57.2 us
    pallas_call x1, Pallas kernels: 59.1 us -> 56.4 us  [body(): pl.pallas_call(kernel, out_shape=(*results,), in_specs=[hbm] * 5 + [pl.Bl...]
where the time goes in v3:
time: 58.6 us; the launch traced here: 58.5 us
  Pallas kernels  57.2 us (98%)
  between operations  1.29 us (2%)
    pallas_call x1, Pallas kernels, body(): pl.pallas_call(kernel, out_shape=(*results,), in_specs=[hbm] * 5 + [pl.Bl...  56.4 us

profile of v3, /device:TPU:8, one launch (start us, length us, event | category | flops | bytes accessed | tf_op | source)
XLA Modules:
  0.0 58.5 jit_solution(6062054324390315180)
XLA Ops:
  1.3 56.4 %shard_map.102 = (bf16[1,2560]{1,0:T(2,128)(2,1)S(1)}, bf16[1,2560]{1,0:T(2,128)(2,1)S(1)}, f32[1,2,128,128]{3,2,1,0:T(8,128)S(1)}, f32[1,2,128,128]{3,2,1,0:T(8,128)S(1)}) custom-call(bf16[128,2560]{1,0:T(8,128)(2,1)} %x_hbm.1, bf16[128,2560]{1,0:T(8,128)(2,1)} %g_hbm.1, bf16[1,2,128,128]{3,2,1,0:T(8,128)(2,1)} %wi_hbm.1, bf16[1,2,128,128]{3,2,1,0:T(8,128)(2,1)} %wo_hbm.1, ...), custom_call_target="tpu_custom_call" | custom-call | tf_op jit(solution)/shard_map/pallas_call | solution.py:410
  57.7 0.7 %shard_map.103 = (bf16[1,2560]{1,0:T(2,128)(2,1)}, bf16[1,2560]{1,0:T(2,128)(2,1)}, f32[1,2,128,128]{3,2,1,0:T(8,128)}, f32[1,2,128,128]{3,2,1,0:T(8,128)}) custom-call(bf16[1,2560]{1,0:T(2,128)(2,1)S(1)} %get-tuple-element.8.refs_0_, bf16[1,2560]{1,0:T(2,128)(2,1)S(1)} %get-tuple-element.9.refs_1_, f32[1,2,128,128]{3,2,1,0:T(8,128)S(1)} %get-tuple-element.10.refs_2_, ...), custom_call_target="tpu_custom_call" | custom-call | tf_op jit(solution)/shard_map/pallas_call | solution.py:468

commit v4 on v3

--- a/solution.py
+++ b/solution.py
@@ -79,9 +79,9 @@
     x_hbm, g_hbm, wi_hbm, wo_hbm, idx_hbm, cnt_ref, seed_hbm,
     out_ref, ing_ref, gwi_ref, gwo_ref,
     x3, g3, x3t, wg, keep_ref, perm_ref, pre_ref, gd_ref, dt_ref, gp_ref,
-    rs_send, rs_recv, c_send, c_recv, own, x_send, x_recv, zsum, z_send, z_recv,
-    idx_ref, seed_ref, idxv, inv,
-    sm_sem, ld_sem, wl_sem, ag_ss, ag_rs, rs_ss, rs_rs, c_ss, c_rs, x_ss, x_rs, z_ss, z_rs, ready,
+    wp, ex_send, ex_recv, rs_send, rs_recv, own, x_send, x_recv, zsum, z_send, z_recv,
+    idx_ref, seed_ref, idxv, inv, idxp, invp,
+    sm_sem, ld_sem, wl_sem, ag_ss, ag_rs, wp_ss, wp_rs, id_sem, ex_ss, ex_rs, rs_ss, rs_rs, x_ss, x_rs, z_ss, z_rs, ready,
 ):
     y = lax.axis_index("dp")
     mp = lax.axis_index("mp")
@@ -129,11 +129,11 @@
         return wrap(y - step if way == 0 else y + step, NY)
 
     def ag_copy(w, step, way, s):
-        slot = 2 * ag_origin(step - 1, way) + s
+        hops = 2 if step == NY // 2 else 1
+        slot = 2 * ag_origin(step - hops, way) + s
         src = w_hbm[w].at[0, s] if step == 1 else wg.at[w, slot]
-        return rdma(
-            src, wg.at[w, slot], ag_ss.at[w], ag_rs.at[w, way, step - 1, s], y_dev[way]
-        )
+        device = at(ag_origin(hops, 1 - way), x, z, core)
+        return rdma(src, wg.at[w, slot], ag_ss.at[w], ag_rs.at[w, way, step - 1, s], device)
 
     def ag_wait(w, step, way, s):
         here = wg.at[w, 2 * ag_origin(step, way) + s]
@@ -141,25 +141,39 @@
             here, here, ag_ss.at[w], ag_rs.at[w, way, step - 1, s], y_dev[way]
         ).wait_recv()
 
+    def pass_on(w, slot):
+        return rdma(wg.at[w, slot], wp.at[w, slot], wp_ss.at[w], wp_rs.at[w], pair_dev)
+
     for w in range(2):
         for s in range(2):
             for way in range(2):
                 ag_copy(w, 1, way, s).start()
+        rdma(
+            w_hbm[w].at[0], wp.at[w, pl.ds(2 * y, 2)], wp_ss.at[w], wp_rs.at[w], pair_dev
+        ).start()
 
     for copy in small:
         copy.wait()
     for k in range(K):
         idxv[k] = jnp.where(k < cnt_ref[0], idx_ref[0, k], NJ)
-    for j in range(NJ):
-        found = jnp.int32(K)
-        for k in range(K):
-            found = jnp.where(idxv[k] == j, k, found)
-        inv[j] = found
+    tables = rdma(idxv, idxp, id_sem.at[0], id_sem.at[1], pair_dev)
+    tables.start()
+
+    def invert(src, dst):
+        for j in range(NJ):
+            found = jnp.int32(K)
+            for k in range(K):
+                found = jnp.where(src[k] == j, k, found)
+            dst[j] = found
+
+    invert(idxv, inv)
     blank = jnp.zeros((BS, BS), BF16)
     x3[NJ] = blank
     g3[NJ] = blank
     wg[0, K] = blank
     wg[1, K] = blank
+    wp[0, K] = blank
+    wp[1, K] = blank
 
     rows = lax.broadcasted_iota(jnp.int32, (BS, BS), 0)
     cols = lax.broadcasted_iota(jnp.int32, (BS, BS), 1)
@@ -206,8 +220,12 @@
             for way in range(2):
                 if s in ag_slots(step, way):
                     ag_wait(w, step, way, s)
-                    if step < NY // 2 and s in ag_slots(step + 1, way):
+                    if step + 1 < NY // 2:
                         ag_copy(w, step + 1, way, s).start()
+                    pass_on(w, 2 * ag_origin(step, way) + s).start()
+        if step == NY // 2 - 2:
+            for way in range(2):
+                ag_copy(w, NY // 2, way, way).start()
 
     pre_ref[...] = pre_part(y)
     gd_ref[...] = gd_part(y)
@@ -220,9 +238,15 @@
         if step == 1:
             for k in range(K):
                 x3t[k] = x3[idxv[k]].T
+        if step == 2:
+            tables.wait()
+            invert(idxp, invp)
         left, right = ag_origin(step, 0), ag_origin(step, 1)
         pre_ref[...] += pre_part(left) + pre_part(right)
         gd_ref[...] += gd_part(left) + gd_part(right)
+
+    def swap(t):
+        return rdma(ex_send.at[t], ex_recv.at[t], ex_ss, ex_rs.at[t], pair_dev)
 
     perm = perm_ref[...]
     keep = keep_ref[...]
@@ -232,31 +256,10 @@
     dropped = (activation * keep).astype(BF16)
     slope = slope * keep
     dt_ref[...] = dropped.T
-    first = mm(perm, dropped).astype(BF16)
-    ag_step(1, NY // 2)
-    grad_pre = ((gd_ref[...] + gd_part(far)) * slope).astype(BF16)
-    gp_ref[...] = grad_pre
-    ordered = (first, mm(perm, grad_pre).astype(BF16))
-
-    def placed(u, lo):
-        t, j = divmod(u, NJ)
-        part = ordered[t][lo:lo + 64]
-        if t == 0:
-            return mm(part, jnp.concatenate((wg[1, inv[j]], wg[1, inv[j + 1]]), axis=1))
-        return mm_t(part, jnp.concatenate((wg[0, inv[j]], wg[0, inv[j + 1]]), axis=0))
-
-    def fill(ref, g, lo):
-        for i in range(0, GROUP, 2):
-            both = placed(g * GROUP + i, lo).astype(ref.dtype)
-            ref[g, i] = both[:, :BS]
-            ref[g, i + 1] = both[:, BS:]
-
-    def c_copy(g):
-        return rdma(c_send.at[g], c_recv.at[g], c_ss, c_rs.at[g], pair_dev)
-
-    def pair_out(g):
-        fill(c_send, g, 0)
-        c_copy(g).start()
+    ordered = mm(perm, dropped).astype(BF16)
+    ex_send[0] = ordered[:64]
+    mine = [ordered[64:]]
+    swap(0).start()
 
     def term(w, slot):
         if w == 1:
@@ -288,17 +291,24 @@
             value = value + rs_recv[w, RS_FLAT[NY // 2, way, s]].astype(F32)
         (gwi_ref, gwo_ref)[w][0, s] = value
 
+    rs_both(1, 1, 0)
+    ag_step(1, NY // 2)
+    grad_pre = ((gd_ref[...] + gd_part(far)) * slope).astype(BF16)
+    gp_ref[...] = grad_pre
+    ordered = mm(perm, grad_pre).astype(BF16)
+    ex_send[1] = ordered[:64]
+    mine.append(ordered[64:])
+    swap(1).start()
+
     def x_copy(g, p):
         sem = x_rs.at[g, min(p, 2)]
         return rdma(x_send.at[g, p], x_recv.at[g, p], x_ss, sem, x_dev[X_WAY[p]])
 
     def x_own(g, sub, chunk):
-        some, span = pl.ds(sub * HALF, HALF), pl.ds(chunk * 16, 16)
-        return own[g, some, span, :] + c_recv[g, some, span, :].astype(F32)
-
-    def x_first(g):
-        c_copy(g).wait_recv()
-        for p in range(4):
+        return own[g, pl.ds(sub * HALF, HALF), pl.ds(chunk * 16, 16), :]
+
+    def x_first(g, pieces):
+        for p in pieces:
             x_send[g, p] = x_own(g, X_SUB[p], X_CHUNK[p]).astype(BF16)
             x_copy(g, p).start()
 
@@ -334,44 +344,69 @@
             t, j = divmod(g * GROUP + i, NJ)
             (out_ref, ing_ref)[t][:, j * BS:(j + 1) * BS] = total[i:i + 1].astype(BF16)
 
-    pair_out(0)
+    both = []
+
+    def product(u):
+        t, j = divmod(u, NJ)
+
+        def pair(j):
+            w = 1 - t
+            return jnp.concatenate((wg[w, inv[j]], wp[w, invp[j]]), axis=t)
+
+        right = jnp.concatenate((pair(j), pair(j + 1)), axis=1 - t)
+        return (mm, mm_t)[t](both[t], right)
+
+    def fill(g):
+        for i in range(0, GROUP, 2):
+            value = product(g * GROUP + i)
+            own[g, i] = value[:, :BS]
+            own[g, i + 1] = value[:, BS:]
+
+    for w in range(2):
+        here = wp.at[w, pl.ds(0, K)]
+        rdma(here, here, wp_ss.at[w], wp_rs.at[w], pair_dev).wait_recv()
+
+    def swap_end(t):
+        swap(t).wait_recv()
+        both.append(jnp.concatenate((mine[t], ex_recv[t]), axis=1))
+
+    rs_both(0, 1, 0)
+    swap_end(0)
+    fill(0)
+    x_first(0, (0, 1))
+    fill(1)
+    x_first(1, (0, 1))
+    swap_end(1)
+    for g in range(2, NG):
+        fill(g)
+        x_first(g, (0, 1))
+    rs_both(1, 2, 1)
+    rs_both(0, 2, 1)
+    for g in range(NG):
+        x_first(g, (2, 3))
+    rs_both(1, 2, 0)
+    x_second(0)
+    rs_both(0, 2, 0)
+    x_second(1)
+    x_second(2)
+    rs_both(1, 3, 1)
+    x_second(3)
+    x_second(4)
+    rs_both(0, 3, 1)
+    z_first(0)
+    rs_both(1, 3, 0)
+    z_first(1)
+    rs_both(0, 3, 0)
+    z_first(2)
+    rs_both(1, 4, 1)
+    z_first(3)
+    rs_both(0, 4, 1)
+    z_first(4)
+    rs_both(1, 4, 0)
+    rs_both(0, 4, 0)
     for w in (1, 0):
-        rs_both(w, 1, 0)
-    pair_out(1)
-    for w in (1, 0):
-        rs_both(w, 2, 1)
-    for g in range(2, NG):
-        pair_out(g)
-    for g in range(NG):
-        fill(own, g, 64)
-    x_first(0)
-    x_first(1)
-    rs_both(1, 2, 0)
-    x_first(2)
-    rs_both(0, 2, 0)
-    x_second(0)
-    x_first(3)
-    rs_both(1, 3, 1)
-    x_second(1)
-    x_first(4)
-    rs_both(0, 3, 1)
-    x_second(2)
-    rs_both(1, 3, 0)
-    z_first(0)
-    rs_both(0, 3, 0)
-    x_second(3)
-    z_first(1)
-    rs_both(1, 4, 1)
-    x_second(4)
-    z_first(2)
-    rs_both(0, 4, 1)
-    rs_both(1, 4, 0)
-    z_first(3)
-    rs_both(0, 4, 0)
-    z_first(4)
-    for w in (1, 0):
+        rs_end(w, 1)
         rs_end(w, 0)
-        rs_end(w, 1)
     for g in range(NG):
         z_end(g)
 
@@ -379,7 +414,9 @@
         here = wg.at[w, pl.ds(0, 14)]
         rdma(here, here, ag_ss.at[w], ag_rs.at[w, 0, 0, 0], y_dev[0]).wait_send()
         rdma(rs_send.at[w], rs_recv.at[w], rs_ss.at[w], rs_rs.at[w, 0], y_dev[0]).wait_send()
-    rdma(c_send, c_recv, c_ss, c_rs.at[0], pair_dev).wait_send()
+        here = wg.at[w, pl.ds(0, K)]
+        rdma(here, here, wp_ss.at[w], wp_rs.at[w], pair_dev).wait_send()
+    rdma(ex_send, ex_recv, ex_ss, ex_rs.at[0], pair_dev).wait_send()
     rdma(x_send, x_recv, x_ss, x_rs.at[0, 0], x_dev[0]).wait_send()
     rdma(
         z_send.at[:, others], z_recv.at[:, others], z_ss, z_rs.at[0], z_dev(1)
@@ -425,10 +462,11 @@
             pltpu.VMEM(block, F32),
             pltpu.VMEM(block, BF16),
             pltpu.VMEM(block, BF16),
+            pltpu.VMEM((2, K + 1, *block), BF16),
+            pltpu.VMEM((2, 64, BS), BF16),
+            pltpu.VMEM((2, 64, BS), BF16),
             pltpu.VMEM((2, 14, *block), BF16),
             pltpu.VMEM((2, 14, *block), BF16),
-            pltpu.VMEM((NG, GROUP, 64, BS), BF16),
-            pltpu.VMEM((NG, GROUP, 64, BS), BF16),
             pltpu.VMEM((NG, GROUP, 64, BS), F32),
             pltpu.VMEM((NG, 6, HALF, 16, BS), BF16),
             pltpu.VMEM((NG, 6, HALF, 16, BS), BF16),
@@ -439,15 +477,20 @@
             pltpu.VMEM((1, BS), jnp.int32),
             pltpu.SMEM((K,), jnp.int32),
             pltpu.SMEM((NJ,), jnp.int32),
+            pltpu.SMEM((K,), jnp.int32),
+            pltpu.SMEM((NJ,), jnp.int32),
             dma((2,)),
             dma((2,)),
             dma((2,)),
             dma((2,)),
             dma((2, 2, 4, 2)),
             dma((2,)),
+            dma((2,)),
+            dma((2,)),
+            dma(()),
+            dma((2,)),
+            dma((2,)),
             dma((2, 14)),
-            dma(()),
-            dma((NG,)),
             dma(()),
             dma((NG, 3)),
             dma(()),

time: 58.6 us -> 56.5 us (0.964)
  the two profiles are of different devices: /device:TPU:8 before, /device:TPU:1 now
where the time goes in v4:
time: 56.5 us; the launch traced here: 56.3 us
  Pallas kernels  55 us (97%)
  between operations  1.29 us (2%)
    pallas_call x1, Pallas kernels, body(): pl.pallas_call(kernel, out_shape=(*results,), in_specs=[hbm] * 5 + [pl.Bl...  54.3 us

profile of v4, /device:TPU:1, one launch (start us, length us, event | category | flops | bytes accessed | tf_op | source)
XLA Modules:
  0.0 56.3 jit_solution(9979152148893510111)
XLA Ops:
  1.3 54.3 %shard_map.102 = (bf16[1,2560]{1,0:T(2,128)(2,1)S(1)}, bf16[1,2560]{1,0:T(2,128)(2,1)S(1)}, f32[1,2,128,128]{3,2,1,0:T(8,128)S(1)}, f32[1,2,128,128]{3,2,1,0:T(8,128)S(1)}) custom-call(bf16[128,2560]{1,0:T(8,128)(2,1)} %x_hbm.1, bf16[128,2560]{1,0:T(8,128)(2,1)} %g_hbm.1, bf16[1,2,128,128]{3,2,1,0:T(8,128)(2,1)} %wi_hbm.1, bf16[1,2,128,128]{3,2,1,0:T(8,128)(2,1)} %wo_hbm.1, ...), custom_call_target="tpu_custom_call" | custom-call | tf_op jit(solution)/shard_map/pallas_call | solution.py:447
  55.6 0.7 %shard_map.103 = (bf16[1,2560]{1,0:T(2,128)(2,1)}, bf16[1,2560]{1,0:T(2,128)(2,1)}, f32[1,2,128,128]{3,2,1,0:T(8,128)}, f32[1,2,128,128]{3,2,1,0:T(8,128)}) custom-call(bf16[1,2560]{1,0:T(2,128)(2,1)S(1)} %get-tuple-element.8.refs_0_, bf16[1,2560]{1,0:T(2,128)(2,1)S(1)} %get-tuple-element.9.refs_1_, f32[1,2,128,128]{3,2,1,0:T(8,128)S(1)} %get-tuple-element.10.refs_2_, ...), custom_call_target="tpu_custom_call" | custom-call | tf_op jit(solution)/shard_map/pallas_call | solution.py:511

commit v5 on v4

--- a/solution.py
+++ b/solution.py
@@ -144,10 +144,11 @@
     def pass_on(w, slot):
         return rdma(wg.at[w, slot], wp.at[w, slot], wp_ss.at[w], wp_rs.at[w], pair_dev)
 
+    for chain in range(2):
+        for w in range(2):
+            for way in range(2):
+                ag_copy(w, 1, way, way ^ chain).start()
     for w in range(2):
-        for s in range(2):
-            for way in range(2):
-                ag_copy(w, 1, way, s).start()
         rdma(
             w_hbm[w].at[0], wp.at[w, pl.ds(2 * y, 2)], wp_ss.at[w], wp_rs.at[w], pair_dev
         ).start()
@@ -215,26 +216,30 @@
     for copy in own_w:
         copy.wait()
 
-    def ag_step(w, step):
-        for s in range(2):
-            for way in range(2):
-                if s in ag_slots(step, way):
-                    ag_wait(w, step, way, s)
-                    if step + 1 < NY // 2:
-                        ag_copy(w, step + 1, way, s).start()
-                    pass_on(w, 2 * ag_origin(step, way) + s).start()
-        if step == NY // 2 - 2:
-            for way in range(2):
-                ag_copy(w, NY // 2, way, way).start()
+    def ag_step(step, weights=(0, 1)):
+        for chain in range(2):
+            for w in weights:
+                for way in range(2):
+                    s = way ^ chain
+                    if s in ag_slots(step, way):
+                        ag_wait(w, step, way, s)
+                        if step + 1 < NY // 2:
+                            ag_copy(w, step + 1, way, s).start()
+                if chain == 0 and step == NY // 2 - 2:
+                    for way in range(2):
+                        ag_copy(w, NY // 2, way, way).start()
+                for way in range(2):
+                    s = way ^ chain
+                    if s in ag_slots(step, way):
+                        pass_on(w, 2 * ag_origin(step, way) + s).start()
 
     pre_ref[...] = pre_part(y)
     gd_ref[...] = gd_part(y)
     for step in range(1, NY // 2):
-        ag_step(0, step)
-        ag_step(1, step)
-        pl.semaphore_wait(ready.at[step - 1], 2)
-        if step < 3:
-            ready_round(step)
+        ag_step(step)
+        if step == NY // 2 - 1:
+            pl.semaphore_wait(ready.at[0], 2)
+            ready_round(1)
         if step == 1:
             for k in range(K):
                 x3t[k] = x3[idxv[k]].T
@@ -251,7 +256,7 @@
     perm = perm_ref[...]
     keep = keep_ref[...]
     far = ag_origin(NY // 2, 0)
-    ag_step(0, NY // 2)
+    ag_step(NY // 2, (0,))
     activation, slope = gelu_parts(pre_ref[...] + pre_part(far))
     dropped = (activation * keep).astype(BF16)
     slope = slope * keep
@@ -292,7 +297,7 @@
         (gwi_ref, gwo_ref)[w][0, s] = value
 
     rs_both(1, 1, 0)
-    ag_step(1, NY // 2)
+    ag_step(NY // 2, (1,))
     grad_pre = ((gd_ref[...] + gd_part(far)) * slope).astype(BF16)
     gp_ref[...] = grad_pre
     ordered = mm(perm, grad_pre).astype(BF16)
@@ -370,6 +375,8 @@
         swap(t).wait_recv()
         both.append(jnp.concatenate((mine[t], ex_recv[t]), axis=1))
 
+    pl.semaphore_wait(ready.at[1], 2)
+    ready_round(2)
     rs_both(0, 1, 0)
     swap_end(0)
     fill(0)
@@ -393,6 +400,7 @@
     x_second(3)
     x_second(4)
     rs_both(0, 3, 1)
+    pl.semaphore_wait(ready.at[2], 2)
     z_first(0)
     rs_both(1, 3, 0)
     z_first(1)

time: 56.5 us -> 56 us (level)
  the two profiles are of different devices: /device:TPU:1 before, /device:TPU:16 now
where the time goes in v5:
time: 56 us; the launch traced here: 55.8 us
  Pallas kernels  54.5 us (97%)
  between operations  1.29 us (2%)
    pallas_call x1, Pallas kernels, body(): pl.pallas_call(kernel, out_shape=(*results,), in_specs=[hbm] * 5 + [pl.Bl...  53.7 us

profile of v5, /device:TPU:16, one launch (start us, length us, event | category | flops | bytes accessed | tf_op | source)
XLA Modules:
  0.0 55.8 jit_solution(14432589795818890498)
XLA Ops:
  1.3 53.7 %shard_map.102 = (bf16[1,2560]{1,0:T(2,128)(2,1)S(1)}, bf16[1,2560]{1,0:T(2,128)(2,1)S(1)}, f32[1,2,128,128]{3,2,1,0:T(8,128)S(1)}, f32[1,2,128,128]{3,2,1,0:T(8,128)S(1)}) custom-call(bf16[128,2560]{1,0:T(8,128)(2,1)} %x_hbm.1, bf16[128,2560]{1,0:T(8,128)(2,1)} %g_hbm.1, bf16[1,2,128,128]{3,2,1,0:T(8,128)(2,1)} %wi_hbm.1, bf16[1,2,128,128]{3,2,1,0:T(8,128)(2,1)} %wo_hbm.1, ...), custom_call_target="tpu_custom_call" | custom-call | tf_op jit(solution)/shard_map/pallas_call | solution.py:455
  55.0 0.7 %shard_map.103 = (bf16[1,2560]{1,0:T(2,128)(2,1)}, bf16[1,2560]{1,0:T(2,128)(2,1)}, f32[1,2,128,128]{3,2,1,0:T(8,128)}, f32[1,2,128,128]{3,2,1,0:T(8,128)}) custom-call(bf16[1,2560]{1,0:T(2,128)(2,1)S(1)} %get-tuple-element.8.refs_0_, bf16[1,2560]{1,0:T(2,128)(2,1)S(1)} %get-tuple-element.9.refs_1_, f32[1,2,128,128]{3,2,1,0:T(8,128)S(1)} %get-tuple-element.10.refs_2_, ...), custom_call_target="tpu_custom_call" | custom-call | tf_op jit(solution)/shard_map/pallas_call | solution.py:519
